TPU v7x, 32 devices: a whole 2x2x4 slice. The times are simulated.
32 devices in a mesh: dp: 16 (over z, y, x), mp: 2 (over core).
Axes of the slice: x: 2, y: 2, z: 4, core: 2. Of those that a mesh axis runs over, the one named last changes fastest.
Arguments:
- images: bfloat16 [32768, 384], P('dp'), may hold values from -6 to 6
- means: float32 [8192, 384], P(('mp', 'dp')), may hold values from -0.6 to 0.6
- precisions: float32 [8192, 384], P(('mp', 'dp')), may hold values from 0.5 to 2
- logits: float32 [8192], replicated, may hold values from -6 to 6
Outputs:
- new_means: float32 [8192, 384], P(('mp', 'dp'))
- new_variances: float32 [8192, 384], P(('mp', 'dp'))
- new_log_weights: float32 [8192], P(('mp', 'dp'))
- log_likelihood: float32 [32768], P('dp')
All inputs are finite; a program needn't handle non-finite values.
Results may differ from a plain program's by a relative error of at most 0.0039.
The roundings to bfloat16 on the way count: a program that leaves them out, or rounds other values in their place, can miss the bound.
Values may be sent and summed in bfloat16 or wider, within the bound.
A program may use at most 128 MiB of HBM per device.

v0:
```python
import functools
import math

import jax
import jax.numpy as jnp
from jax import lax
from jax.experimental import pallas as pl
from jax.experimental.pallas import tpu as pltpu
from jax.sharding import Mesh, PartitionSpec as P

MESH = pl.DeviceIdType.MESH
SQUARE = 4
PIECES = 2
F32 = jnp.float32
BF16 = jnp.bfloat16
VMEM_LIMIT = 60 * 1024 * 1024


def remote(src, dst, send, recv, device):
    return pltpu.make_async_remote_copy(
        src_ref=src, dst_ref=dst, send_sem=send, recv_sem=recv, device_id=device, device_id_type=MESH
    )


def features(x):
    wide = x.astype(F32)
    return jnp.concatenate([(wide * wide).astype(BF16), x], axis=1)


def target(k, a, n):
    left, right = a, n - 1 - a
    far, near = jnp.maximum(left, right), jnp.minimum(left, right)
    lead = far - near
    late = jnp.maximum(k - lead, 0)
    dist = jnp.where(k < lead, far - k, near - late // 2)
    to_far = jnp.logical_or(k < lead, lax.rem(late, 2) == 0)
    to_right = jnp.where(right >= left, to_far, jnp.logical_not(to_far))
    return jnp.where(to_right, a + dist, a - dist)


def score_kernel(n_ca, img_ref, w_ref, off_ref, imgs_out, e_out, peak_ref, lse_ref,
                 imgs, wall, offall, ebuf, blk_lse, loc, isend, irecv,
                 wsend, wrecv, osend, orecv, esem, psem):
    a, b, m = lax.axis_index("ca"), lax.axis_index("ib"), lax.axis_index("mp")
    t_rows = img_ref.shape[0]
    r = w_ref.shape[0]
    core = lax.rem(m, 2)
    partner = m + 1 - 2 * core
    bx = b + 1 - 2 * lax.rem(b, 2)
    by = lax.rem(b + 2, 4)
    bd = lax.rem(bx + 2, 4)
    to_x, to_y, to_p = (a, bx, m), (a, by, m), (a, b, partner)
    sub = t_rows // (2 * PIECES)

    barrier = pltpu.get_barrier_semaphore()
    for dev in (to_x, to_y, to_p):
        pl.semaphore_signal(barrier, inc=1, device_id=dev, device_id_type=MESH)

    @pl.when(a > 0)
    def _():
        pl.semaphore_signal(barrier, inc=1, device_id=(a - 1, b, m), device_id_type=MESH)

    @pl.when(a < n_ca - 1)
    def _():
        pl.semaphore_signal(barrier, inc=1, device_id=(a + 1, b, m), device_id_type=MESH)

    own = (
        pltpu.make_async_copy(img_ref, imgs.at[b], loc.at[0]),
        pltpu.make_async_copy(w_ref, wall.at[a], loc.at[1]),
        pltpu.make_async_copy(off_ref, offall.at[a], loc.at[2]),
    )
    for c in own:
        c.start()
    ends = (a == 0).astype(jnp.int32) + (a == n_ca - 1).astype(jnp.int32)
    pl.semaphore_wait(barrier, 5 - ends)

    def img_copy(k, i, dev, piece, first=False):
        rows = pl.ds(pl.multiple_of((core * PIECES + piece) * sub, sub), sub)
        dst = imgs.at[i, rows]
        return remote(img_ref.at[rows] if first else dst, dst, isend.at[k, piece], irecv.at[k, piece], dev)

    def chain(way, s, blk, first=False):
        blk = jnp.clip(blk, 0, n_ca - 1)
        dev = (jnp.clip(a + 1 - 2 * way, 0, n_ca - 1), b, m)
        return (
            remote(w_ref if first else wall.at[blk], wall.at[blk], wsend.at[way, s], wrecv.at[way, s], dev),
            remote(off_ref if first else offall.at[blk], offall.at[blk], osend.at[way, s], orecv.at[way, s], dev),
        )

    def has_next(way):
        return jnp.where(way == 0, a < n_ca - 1, a > 0)

    for way in (0, 1):
        @pl.when(has_next(way))
        def _():
            for c in chain(way, 0, a, True):
                c.start()

    for piece in range(PIECES):
        img_copy(0, b, to_x, piece, True).start()
        img_copy(1, b, to_y, piece, True).start()
    for c in own:
        c.wait()

    def place(q):
        j = target(n_ca - 1 - q, a, n_ca)
        return j, (j > a).astype(jnp.int32)

    def take(q):
        j, way = place(q)
        s = jnp.maximum(jnp.abs(a - j) - 1, 0)
        for c in chain(way, s, j):
            c.wait_recv()

        @pl.when(has_next(way))
        def _():
            for c in chain(way, s + 1, j):
                c.start()

    def images_in(piece):
        img_copy(0, bx, to_x, piece).wait_recv()
        img_copy(3, bx, to_p, piece).start()

        @pl.when(core == 0)
        def _():
            img_copy(2, bx, to_y, piece).start()

        img_copy(1, by, to_y, piece).wait_recv()
        img_copy(4, by, to_p, piece).start()

        @pl.when(core == 1)
        def _():
            img_copy(2, by, to_x, piece).start()

    def corner_in(piece):
        img_copy(2, bd, to_x, piece).wait_recv()
        img_copy(5, bd, to_p, piece).start()

    def paired(k, i):
        for piece in range(PIECES):
            img_copy(k, i, to_p, piece).wait_recv()

    def put(i, slot):
        return pltpu.make_async_copy(imgs.at[i], imgs_out.at[i], psem.at[slot])

    def shard(p):
        return jnp.where(p == 0, b, jnp.where(p == 1, bx, jnp.where(p == 2, by, bd)))

    near = n_ca - 1

    def e_copy(t, j, i):
        slot = lax.rem(t, 2)
        rows = pl.ds(pl.multiple_of(j * r, r), r)
        cols = pl.ds(pl.multiple_of(i * t_rows, t_rows), t_rows)
        return pltpu.make_async_copy(ebuf.at[slot], e_out.at[rows, cols], esem.at[slot])

    @pl.loop(0, 4 * n_ca)
    def _(t):
        p = jnp.where(t < 3 * near, t // near, jnp.where(t < 3 * n_ca, t - 3 * near, 3))
        q = jnp.where(t < 3 * near, lax.rem(t, near), jnp.where(t < 3 * n_ca, near, t - 3 * n_ca))

        @pl.when(t == near - 1)
        def _():
            for piece in range(PIECES - 1):
                images_in(piece)

        @pl.when(jnp.logical_and(t >= 1, t < near))
        def _():
            take(jnp.clip(t, 1, near))

        @pl.when(t == near)
        def _():
            put(b, 0).start()
            images_in(PIECES - 1)

            @pl.when(has_next(place(near)[1]))
            def _():
                take(near)

            paired(3, bx)

        @pl.when(t == 2 * near)
        def _():
            put(bx, 1).start()
            for piece in range(PIECES - 1):
                corner_in(piece)
            paired(4, by)

        @pl.when(t == 3 * near)
        def _():
            put(by, 2).start()
            corner_in(PIECES - 1)

            @pl.when(jnp.logical_not(has_next(place(near)[1])))
            def _():
                take(near)

        @pl.when(t == 3 * n_ca)
        def _():
            paired(5, bd)
            put(bd, 3).start()

        i = shard(p)
        j = place(q)[0]

        @pl.when(t >= 2)
        def _():
            e_copy(t, j, i).wait()

        cols = pl.ds(pl.multiple_of(i * t_rows, t_rows), t_rows)
        feats = features(imgs[i])
        s = lax.dot_general(wall[j], feats, (((1,), (1,)), ((), ())), preferred_element_type=F32)
        column = jnp.broadcast_to(offall[j], (128, r)).T
        s = s + column[:, :1]
        peak = jnp.max(s, axis=0, keepdims=True)
        e = jnp.exp(s - peak)
        ebuf[lax.rem(t, 2)] = e
        peak_ref[j, :, cols] = peak
        blk_lse[j, :, cols] = peak + jnp.log(jnp.sum(e, axis=0, keepdims=True))
        e_copy(t, j, i).start()

    high = lax.fori_loop(1, n_ca, lambda k, h: jnp.maximum(h, blk_lse[k]), blk_lse[0])
    tot = lax.fori_loop(1, n_ca, lambda k, x: x + jnp.exp(blk_lse[k] - high), jnp.exp(blk_lse[0] - high))
    lse_ref[...] = high + jnp.log(tot)

    for t in (0, 1):
        e_copy(t, a, b).wait()
    for slot, i in enumerate((b, bx, by, bd)):
        put(i, slot).wait()
    for k, i in enumerate((b, b, bd, bx, by, bd)):
        for piece in range(PIECES):
            img_copy(k, i, to_p, piece).wait_send()
    for way in (0, 1):
        @pl.loop(0, n_ca - 1)
        def _(s):
            blk = a - s + 2 * way * s
            ok = jnp.logical_and(has_next(way), jnp.logical_and(blk >= 0, blk < n_ca))

            @pl.when(ok)
            def _():
                for c in chain(way, s, blk):
                    c.wait_send()


def score(images, w, off, n_ca):
    t, d = images.shape
    r = w.shape[0]
    rows = SQUARE * t
    any_spec = pl.BlockSpec(memory_space=pl.ANY)
    vmem = pl.BlockSpec(memory_space=pltpu.VMEM)
    dma = pltpu.SemaphoreType.DMA
    line = dma((2, n_ca - 1))
    return pl.pallas_call(
        functools.partial(score_kernel, n_ca),
        out_shape=(
            jax.ShapeDtypeStruct((SQUARE, t, d), BF16),
            jax.ShapeDtypeStruct((n_ca * r, rows), F32),
            jax.ShapeDtypeStruct((n_ca, 1, rows), F32),
            jax.ShapeDtypeStruct((1, rows), F32),
        ),
        in_specs=[any_spec, vmem, vmem],
        out_specs=(any_spec, any_spec, vmem, vmem),
        scratch_shapes=[
            pltpu.VMEM((SQUARE, t, d), BF16),
            pltpu.VMEM((n_ca, r, 2 * d), BF16),
            pltpu.VMEM((n_ca, 1, r), F32),
            pltpu.VMEM((2, r, t), F32),
            pltpu.VMEM((n_ca, 1, rows), F32),
            dma((3,)),
            dma((6, PIECES)),
            dma((6, PIECES)),
            line, line, line, line,
            dma((2,)),
            dma((4,)),
        ],
        compiler_params=pltpu.CompilerParams(
            collective_id=0, has_side_effects=True, vmem_limit_bytes=VMEM_LIMIT
        ),
        name="score",
    )(images, w, off)


def lse_kernel(n_mp, lse_ref, peak_ref, logits_ref, factor_ref, like_ref, buf, send, recv):
    a, b, m = lax.axis_index("ca"), lax.axis_index("ib"), lax.axis_index("mp")
    n = SQUARE * n_mp
    me = b * n_mp + m

    def device(k):
        p = lax.rem(me + k, n)
        return (a, p // n_mp, lax.rem(p, n_mp))

    barrier = pltpu.get_barrier_semaphore()

    @pl.loop(1, n)
    def _(k):
        pl.semaphore_signal(barrier, inc=1, device_id=device(k), device_id_type=MESH)

    pl.semaphore_wait(barrier, n - 1)

    def copy(k):
        return remote(lse_ref, buf.at[k], send.at[k], recv.at[k], device(k))

    @pl.loop(1, n)
    def _(k):
        copy(k).start()

    logits = logits_ref[...]
    top = jnp.max(logits, axis=1, keepdims=True)
    logit_total = top + jnp.log(jnp.sum(jnp.exp(logits - top), axis=1, keepdims=True))

    @pl.loop(1, n)
    def _(k):
        copy(k).wait()

    own = lse_ref[...]
    high = lax.fori_loop(1, n, lambda k, h: jnp.maximum(h, buf[k]), own)
    total = lax.fori_loop(1, n, lambda k, t: t + jnp.exp(buf[k] - high), jnp.exp(own - high))
    row_total = high + jnp.log(total)
    factor_ref[...] = jnp.exp(peak_ref[...] - row_total[None])
    like_ref[...] = row_total - logit_total


def combine(lse, peak, logits, n_mp):
    n = SQUARE * n_mp
    vmem = pl.BlockSpec(memory_space=pltpu.VMEM)
    return pl.pallas_call(
        functools.partial(lse_kernel, n_mp),
        out_shape=(jax.ShapeDtypeStruct(peak.shape, F32), jax.ShapeDtypeStruct(lse.shape, F32)),
        in_specs=[vmem] * 3,
        out_specs=(vmem,) * 2,
        scratch_shapes=[
            pltpu.VMEM((n,) + lse.shape, F32),
            pltpu.SemaphoreType.DMA((n,)),
            pltpu.SemaphoreType.DMA((n,)),
        ],
        compiler_params=pltpu.CompilerParams(collective_id=1, has_side_effects=True),
        name="combine",
    )(lse, peak, logits[None, :])


def moment_kernel(n_ca, x_ref, e_ref, factor_ref, means_ref, prec_ref,
                  nm_ref, nv_ref, nw_ref, acc, cacc, crow, sbuf, sc, rbuf, rc,
                  msend, mrecv, csend, crecv):
    a, b, m = lax.axis_index("ca"), lax.axis_index("ib"), lax.axis_index("mp")
    k, i = pl.program_id(0), pl.program_id(1)
    last = pl.num_programs(1) - 1
    d = means_ref.shape[1]
    barrier = pltpu.get_barrier_semaphore()

    @pl.when(jnp.logical_and(k == 0, i == 0))
    def _():
        @pl.when(a > 0)
        def _():
            pl.semaphore_signal(barrier, inc=1, device_id=(a - 1, b, m), device_id_type=MESH)

        @pl.when(a < n_ca - 1)
        def _():
            pl.semaphore_signal(barrier, inc=1, device_id=(a + 1, b, m), device_id_type=MESH)

        ends = (a == 0).astype(jnp.int32) + (a == n_ca - 1).astype(jnp.int32)
        pl.semaphore_wait(barrier, 2 - ends)

    def copies(j, way):
        nbr = jnp.clip(a + 1 - 2 * way, 0, n_ca - 1)
        dev = (nbr, b, m)
        return (
            remote(sbuf.at[j], rbuf.at[way, j], msend.at[j], mrecv.at[way, j], dev),
            remote(sc.at[j], rc.at[way, j], csend.at[j], crecv.at[way, j], dev),
        )

    def info(q):
        j = target(q, a, n_ca)
        way = (j < a).astype(jnp.int32)
        joined = jnp.where(j < a, a < n_ca - 1, a > 0)
        return j, way, joined

    def start(q):
        j, way, _ = info(q)
        for c in copies(j, way):
            c.start()

    def merge(q):
        j, way, _ = info(q)
        for c in copies(j, way):
            c.wait_recv()
        sbuf[j] = (acc[q] + rbuf[way, j].astype(F32)).astype(BF16)
        sc[j] = crow[q] + rc[way, j]

    @pl.when(jnp.logical_and(i == 0, k >= 1))
    def _():
        @pl.when(jnp.logical_not(info(k - 1)[2]))
        def _():
            start(k - 1)

        @pl.when(jnp.logical_and(k >= 2, info(jnp.maximum(k - 2, 0))[2]))
        def _():
            start(k - 2)

    feats = features(x_ref[...])
    shares = (e_ref[...] * factor_ref[0]).astype(BF16)
    wide = shares.astype(F32)
    part = wide[:, :128]
    for q in range(1, wide.shape[1] // 128):
        part = part + wide[:, q * 128:(q + 1) * 128]
    prod = jnp.dot(shares, feats, preferred_element_type=F32)

    @pl.when(i == 0)
    def _():
        acc[k] = prod
        cacc[...] = part

    @pl.when(i > 0)
    def _():
        acc[k] += prod
        cacc[...] += part

    @pl.when(i == last)
    def _():
        crow[k] = jnp.sum(cacc[...].T, axis=0, keepdims=True)

        @pl.when(jnp.logical_and(k < n_ca - 1, jnp.logical_not(info(k)[2])))
        def _():
            j = info(k)[0]
            sbuf[j] = acc[k].astype(BF16)
            sc[j] = crow[k]

        @pl.when(jnp.logical_and(k >= 1, info(jnp.maximum(k - 1, 0))[2]))
        def _():
            merge(k - 1)

        @pl.when(k == n_ca - 1)
        def _():
            means, prec = means_ref[...], prec_ref[...]
            nm_ref[...] = acc[n_ca - 1, :, d:] + means
            nv_ref[...] = acc[n_ca - 1, :, :d] + 1.0 / prec + means * means

            @pl.when(info(n_ca - 2)[2])
            def _():
                start(n_ca - 2)

            def join(way):
                for c in copies(a, way):
                    c.wait_recv()
                nm_ref[...] += rbuf[way, a, :, d:].astype(F32)
                nv_ref[...] += rbuf[way, a, :, :d].astype(F32)
                crow[n_ca - 1] += rc[way, a]

            @pl.when(a > 0)
            def _():
                join(0)

            @pl.when(a < n_ca - 1)
            def _():
                join(1)

            denominator = crow[n_ca - 1] + 1.0
            nw_ref[...] = denominator

            @pl.loop(0, n_ca - 1)
            def _(q):
                j, way, _ = info(q)
                for c in copies(j, way):
                    c.wait_send()


def moment(x, e, factor, means, precisions, n_ca):
    rows, d = x.shape
    r = means.shape[0]
    n = min(2048, rows)
    dma = pltpu.SemaphoreType.DMA
    fixed = lambda k, i: (0, 0)

    def e_map(k, i):
        return target(k, lax.axis_index("ca"), n_ca), i

    def f_map(k, i):
        return target(k, lax.axis_index("ca"), n_ca), 0, i

    return pl.pallas_call(
        functools.partial(moment_kernel, n_ca),
        grid=(n_ca, rows // n),
        out_shape=(
            jax.ShapeDtypeStruct((r, d), F32),
            jax.ShapeDtypeStruct((r, d), F32),
            jax.ShapeDtypeStruct((1, r), F32),
        ),
        in_specs=[
            pl.BlockSpec((n, d), lambda k, i: (i, 0)),
            pl.BlockSpec((r, n), e_map),
            pl.BlockSpec((1, 1, n), f_map),
            pl.BlockSpec((r, d), fixed),
            pl.BlockSpec((r, d), fixed),
        ],
        out_specs=(
            pl.BlockSpec((r, d), fixed),
            pl.BlockSpec((r, d), fixed),
            pl.BlockSpec((1, r), fixed),
        ),
        scratch_shapes=[
            pltpu.VMEM((n_ca, r, 2 * d), F32),
            pltpu.VMEM((r, 128), F32),
            pltpu.VMEM((n_ca, 1, r), F32),
            pltpu.VMEM((n_ca, r, 2 * d), BF16),
            pltpu.VMEM((n_ca, 1, r), F32),
            pltpu.VMEM((2, n_ca, r, 2 * d), BF16),
            pltpu.VMEM((2, n_ca, 1, r), F32),
            dma((n_ca,)),
            dma((2, n_ca)),
            dma((n_ca,)),
            dma((2, n_ca)),
        ],
        compiler_params=pltpu.CompilerParams(
            collective_id=2, has_side_effects=True, vmem_limit_bytes=VMEM_LIMIT
        ),
        name="moment",
    )(x, e, factor, means, precisions)


def body(n_ca, n_mp, images, means, precisions, logits):
    t, d = images.shape
    r = means.shape[0]
    a, b, m = lax.axis_index("ca"), lax.axis_index("ib"), lax.axis_index("mp")
    own_logits = lax.dynamic_slice_in_dim(logits, ((m * n_ca + a) * SQUARE + b) * r, r)
    prec_b = precisions.astype(BF16)
    w = jnp.concatenate([-0.5 * prec_b, (means * precisions).astype(BF16)], axis=1)
    off = (
        own_logits
        + 0.5 * jnp.sum(jnp.log(precisions) - means * means * precisions, axis=1)
        - 0.5 * d * math.log(2.0 * math.pi)
    )
    imgs, e, peak, lse = score(images, w, off[None, :], n_ca)
    x = imgs.reshape(SQUARE * t, d)
    factor, like = combine(lse, peak, logits, n_mp)
    log_likelihood = lax.dynamic_slice_in_dim(like[0], b * t, t)
    total = float(t * n_ca * SQUARE + logits.shape[0])
    first, second, denominator = moment(x, e, factor, means, precisions, n_ca)
    denominator = denominator[0]
    new_means = first / denominator[:, None]
    new_variances = second / denominator[:, None] - new_means * new_means
    new_log_weights = jnp.log(denominator) - jnp.log(jnp.float32(total))
    return (new_means, new_variances, new_log_weights, log_likelihood)


def solution(mesh):
    n_dp, n_mp = mesh.shape["dp"], mesh.shape["mp"]
    n_ca = n_dp // SQUARE
    split = Mesh(mesh.devices.reshape(n_ca, SQUARE, n_mp), ("ca", "ib", "mp"))
    dp = ("ca", "ib")
    comp = ("mp", "ca", "ib")
    return jax.shard_map(
        functools.partial(body, n_ca, n_mp),
        mesh=split,
        in_specs=(P(dp, None), P(comp, None), P(comp, None), P()),
        out_specs=(P(comp, None), P(comp, None), P(comp), P(dp)),
        check_vma=False,
    )
```

profile of v0, /device:TPU:16, one launch (start us, length us, event | category | flops | bytes accessed | tf_op | source)
XLA Modules:
  0.0 112.6 jit_solution(10985726625225095268)
XLA Ops:
  0.6 1.0 convert_multiply_fusion
  1.7 1.3 %subtract_reduce_fusion = (f32[256]{0:T(256)S(1)}, bf16[256,384]{1,0:T(8,128)(2,1)S(1)}) fusion(f32[256,384]{1,0:T(8,128)} %prec_ref.1, f32[256,384]{1,0:T(8,128)} %means_ref.1), kind=kLoop, calls=%fused_computation.2 | loop fusion | flops 589568 | bytes 984064 | tf_op jit(solution)/shard_map/reduce_sum | solution.py:528
  3.0 1.3 %add_add_fusion = f32[256]{0:T(256)} fusion(f32[256]{0:T(256)S(1)} %get-tuple-element.24, f32[8192]{0:T(1024)} %param.7, s32[]{:T(128)S(6)} %select_n.6), kind=kLoop, calls=%fused_computation.7 | loop fusion | flops 768 | bytes 3076 | tf_op jit(solution)/shard_map/sub | solution.py:527
  4.3 0.8 pad_maximum_fusion.w_ref
  5.1 44.9 %score.1 = (bf16[4,2048,384]{2,1,0:T(8,128)(2,1)}, f32[1024,8192]{1,0:T(8,128)}, f32[4,1,8192]{2,1,0:T(1,128)}, f32[1,8192]{1,0:T(1,128)}) custom-call(bf16[2048,384]{1,0:T(8,128)(2,1)} %img_ref.1, bf16[256,768]{1,0:T(8,128)(2,1)} %pad_maximum_fusion.w_ref, f32[1,256]{1,0:T(1,128)} %bitcast.8), custom_call_target="tpu_custom_call" | custom-call | tf_op jit(solution)/shard_map/score/pallas_call | solution.py:253
  50.0 9.6 %combine.1 = (f32[4,1,8192]{2,1,0:T(1,128)}, f32[1,8192]{1,0:T(1,128)}) custom-call(f32[1,8192]{1,0:T(1,128)} %get-tuple-element.15.lse_ref, f32[4,1,8192]{2,1,0:T(1,128)} %get-tuple-element.16.peak_ref, f32[1,8192]{1,0:T(1,128)} %bitcast.6), custom_call_target="tpu_custom_call" | custom-call | tf_op jit(solution)/shard_map/combine/pallas_call | solution.py:326
  59.6 48.4 %moment.1 = (f32[256,384]{1,0:T(8,128)}, f32[256,384]{1,0:T(8,128)}, f32[1,256]{1,0:T(1,128)}) custom-call(bf16[8192,384]{1,0:T(8,128)(2,1)} %bitcast.5, f32[1024,8192]{1,0:T(8,128)} %get-tuple-element.14.e_ref, f32[4,1,8192]{2,1,0:T(1,128)} %get-tuple-element.17.factor_ref, f32[256,384]{1,0:T(8,128)} %means_ref.1, f32[256,384]{1,0:T(8,128)} %prec_ref.1), custom_call_target="tpu_custom_call" | custom-call | tf_op jit(solution)/shard_map/moment/pallas_call | solution.py:479
  108.0 2.1 %multiply_subtract_fusion = (f32[256,384]{1,0:T(8,128)}, f32[256,384]{1,0:T(8,128)}) fusion(f32[256,384]{1,0:T(8,128)} %get-tuple-element.20, f32[256]{0:T(256)} %bitcast.9, f32[256,384]{1,0:T(8,128)} %get-tuple-element.18), kind=kLoop, calls=%fused_computation.1 | loop fusion | flops 393216 | bytes 1573888 | tf_op jit(solution)/shard_map/sub | solution.py:539
  110.1 1.2 %log_add_fusion = f32[256]{0:T(256)} fusion(f32[256]{0:T(256)} %bitcast.10), kind=kLoop, calls=%fused_computation.6 | loop fusion | flops 256 | bytes 2048 | tf_op jit(solution)/shard_map/sub | solution.py:540
  111.3 1.3 %constant_dynamic-slice_fusion = f32[1,2048]{1,0:T(1,128)} fusion(f32[1,8192]{1,0:T(1,128)} %get-tuple-element.21, s32[]{:T(128)S(6)} %select_n.7), kind=kLoop, calls=%fused_computation.8 | loop fusion | bytes 16388 | tf_op jit(solution)/shard_map/dynamic_slice | solution.py:534
where the time goes:
time: 114 us; the launch traced here: 113 us
  Pallas kernels  103 us (90%)
  other arithmetic  7.81 us (7%)
  local copies, waits for them, and re-layouts  1.29 us (1%)
    pallas_call x1, Pallas kernels, moment(): pl.pallas_call(functools.partial(moment_kernel, n_ca), grid=(n_ca, rows /...  48.4 us
    pallas_call x1, Pallas kernels, score(): pl.pallas_call(functools.partial(score_kernel, n_ca), out_shape=(jax.Shap...  44.9 us
    pallas_call x1, Pallas kernels, combine(): pl.pallas_call(functools.partial(lse_kernel, n_mp), out_shape=(jax.ShapeD...  9.59 us

commit v1 on v0

v1 whole, which is shorter than its diff:
```python
import functools
import math

import jax
import jax.numpy as jnp
from jax import lax
from jax.experimental import pallas as pl
from jax.experimental.pallas import tpu as pltpu
from jax.sharding import Mesh, PartitionSpec as P

MESH = pl.DeviceIdType.MESH
SQUARE = 4
PIECES = 2
TILES = 2
F32 = jnp.float32
BF16 = jnp.bfloat16
VMEM_LIMIT = 67_043_328


def remote(src, dst, send, recv, device):
    return pltpu.make_async_remote_copy(
        src_ref=src, dst_ref=dst, send_sem=send, recv_sem=recv, device_id=device, device_id_type=MESH
    )


def target(k, a, n):
    left, right = a, n - 1 - a
    far, near = jnp.maximum(left, right), jnp.minimum(left, right)
    lead = far - near
    late = jnp.maximum(k - lead, 0)
    dist = jnp.where(k < lead, far - k, near - late // 2)
    to_far = jnp.logical_or(k < lead, lax.rem(late, 2) == 1)
    to_right = jnp.where(right >= left, to_far, jnp.logical_not(to_far))
    return jnp.where(to_right, a + dist, a - dist)


def schedule(n_ca):
    b, c = n_ca - 2, n_ca - 1
    both, near, far, early, late = (0, 4), (1, 1), (5, 1), (0, 1), (4, 1)
    shapes = (
        (0, 1, both, 2),
        (1, b, both, 2),
        (0, b, near, 2),
        (b, c, both, 2),
        (b, c, near, 2),
        (0, c, far, 2),
        (0, c, (3, 1), 1),
        (c, n_ca, early, 4),
        (0, c, (7, 1), 1),
        (c, n_ca, late, 4),
    )
    out, t = [], 0
    for q0, q1, (p0, stride), count in shapes:
        out.append((t, q0, p0, stride, count))
        t += (q1 - q0) * count
    return out, t


def em_kernel(n_ca, n_mp, halves, img_ref, means_ref, prec_ref, logits_ref,
              first_ref, second_ref, den_ref, like_ref,
              feats, wall, offall, ebuf, peak, blk_lse, lse, tot, lbuf, acc, cacc, crow, sbuf, sc, rbuf, rc,
              loc, isend, irecv, wsend, wrecv, osend, orecv, lsend, lrecv, msend, mrecv, csend, crecv):
    a, b, m = lax.axis_index("ca"), lax.axis_index("ib"), lax.axis_index("mp")
    t_rows, d = img_ref.shape
    r = means_ref.shape[0]
    rh = r // halves
    core = lax.rem(m, 2)
    partner = m + 1 - 2 * core
    bx = b + 1 - 2 * lax.rem(b, 2)
    by = lax.rem(b + 2, 4)
    bd = lax.rem(bx + 2, 4)
    to_x, to_y, to_p = (a, bx, m), (a, by, m), (a, b, partner)
    sub = t_rows // (2 * PIECES)
    part_rows = 2 * sub
    n = SQUARE * n_mp
    me = b * n_mp + m

    def peer(k):
        p = lax.rem(me + k, n)
        return (a, p // n_mp, lax.rem(p, n_mp))

    barrier = pltpu.get_barrier_semaphore()

    @pl.loop(1, n)
    def _(k):
        pl.semaphore_signal(barrier, inc=1, device_id=peer(k), device_id_type=MESH)

    @pl.when(a > 0)
    def _():
        pl.semaphore_signal(barrier, inc=1, device_id=(a - 1, b, m), device_id_type=MESH)

    @pl.when(a < n_ca - 1)
    def _():
        pl.semaphore_signal(barrier, inc=1, device_id=(a + 1, b, m), device_id_type=MESH)

    def image_cols(i, rows):
        return feats.at[i, rows, pl.ds(d, d)]

    own = pltpu.make_async_copy(img_ref, feats.at[b, :, pl.ds(d, d)], loc.at[0])
    own.start()

    means, prec = means_ref[...], prec_ref[...]
    wall[a] = jnp.concatenate([-0.5 * prec.astype(BF16), (means * prec).astype(BF16)], axis=1)
    terms = 0.5 * jnp.sum(jnp.log(prec) - means * means * prec, axis=1, keepdims=True)
    row = jnp.broadcast_to(terms, (r, 128)).T[:1]
    offall[a] = logits_ref[(m * n_ca + a) * SQUARE + b] + row - 0.5 * d * math.log(2.0 * math.pi)

    ends = (a == 0).astype(jnp.int32) + (a == n_ca - 1).astype(jnp.int32)
    pl.semaphore_wait(barrier, n + 1 - ends)

    def img_copy(k, i, dev, piece, first=False):
        rows = pl.ds(pl.multiple_of((piece * 2 + core) * sub, sub), sub)
        dst = image_cols(i, rows)
        return remote(img_ref.at[rows] if first else dst, dst, isend.at[k, piece], irecv.at[k, piece], dev)

    def has_next(way):
        return a < n_ca - 1 if way == 0 else a > 0

    def hop(way, dist, sender):
        blk = jnp.clip(sender - dist + 2 * way * dist, 0, n_ca - 1)
        return blk, (jnp.clip(a + 1 - 2 * way, 0, n_ca - 1), b, m)

    def w_copy(way, dist, h, sender):
        blk, dev = hop(way, dist, sender)
        block = wall.at[blk, pl.ds(h * rh, rh)]
        return remote(block, block, wsend.at[way, dist, h], wrecv.at[way, dist, h], dev)

    def off_copy(way, dist, sender):
        blk, dev = hop(way, dist, sender)
        return remote(offall.at[blk], offall.at[blk], osend.at[way, dist], orecv.at[way, dist], dev)

    def exists(way, dist):
        blk = a - dist + 2 * way * dist
        return jnp.logical_and(blk >= 0, blk < n_ca)

    def forward(way, dist, h):
        @pl.when(has_next(way))
        def _():
            w_copy(way, dist, h, a).start()
            if h == 0:
                off_copy(way, dist, a).start()

    for piece in range(PIECES):
        img_copy(0, b, to_x, piece, True).start()
        img_copy(1, b, to_y, piece, True).start()
    for h in range(halves):
        for way in (0, 1):
            forward(way, 0, h)

    def event(u):
        dist, h = u // halves + 1, u % halves
        for way in (0, 1):
            @pl.when(exists(way, dist))
            def _():
                sender = a - 1 + 2 * way
                w_copy(way, dist - 1, h, sender).wait_recv()
                if h == 0:
                    off_copy(way, dist - 1, sender).wait_recv()
                if dist < n_ca - 1:
                    forward(way, dist, h)

    def images_in(piece):
        img_copy(0, bx, to_x, piece).wait_recv()
        img_copy(3, bx, to_p, piece).start()

        @pl.when(core == 0)
        def _():
            img_copy(2, bx, to_y, piece).start()

        img_copy(1, by, to_y, piece).wait_recv()
        img_copy(4, by, to_p, piece).start()

        @pl.when(core == 1)
        def _():
            img_copy(2, by, to_x, piece).start()

    def corner_in(piece):
        img_copy(2, bd, to_x, piece).wait_recv()
        img_copy(5, bd, to_p, piece).start()

    def square(i, piece):
        rows = pl.ds(pl.multiple_of(piece * part_rows, part_rows), part_rows)
        wide = feats[i, rows, d:].astype(F32)
        feats[i, rows, :d] = (wide * wide).astype(BF16)

    def paired(k, i, piece):
        img_copy(k, i, to_p, piece).wait_recv()
        square(i, piece)

    own.wait()
    for piece in range(PIECES):
        square(b, piece)

    def shard(p):
        return jnp.where(p == 0, b, jnp.where(p == 1, bx, jnp.where(p == 2, by, bd)))

    def send_lse(k, hh):
        return remote(lse.at[hh], lbuf.at[k, hh], lsend.at[k, hh], lrecv.at[k, hh], peer(k))

    def reduce_lse(hh):
        high = lax.fori_loop(1, n_ca, lambda k, h: jnp.maximum(h, blk_lse[k, hh]), blk_lse[0, hh])
        tot = lax.fori_loop(
            1, n_ca, lambda k, x: x + jnp.exp(blk_lse[k, hh] - high), jnp.exp(blk_lse[0, hh] - high)
        )
        lse[hh] = high + jnp.log(tot)

    def share_lse(hh):
        @pl.loop(1, n)
        def _(k):
            send_lse(k, hh).start()

    rects, tiles = schedule(n_ca)
    pair = [x[0] // TILES for x in rects]
    events = (n_ca - 1) * halves

    def tile(t):
        q, part = t, t
        for t0, q0, p0, stride, count in rects:
            here = t >= t0
            s = jnp.maximum(t - t0, 0)
            q = jnp.where(here, q0 + s // count, q)
            part = jnp.where(here, p0 + stride * lax.rem(s, count), part)
        j = target(n_ca - 1 - q, a, n_ca)
        hh = part // SQUARE
        i = shard(part - SQUARE * hh)
        cols = pl.ds(pl.multiple_of(hh * part_rows, part_rows), part_rows)
        s = lax.dot_general(wall[j], feats[i, cols], (((1,), (1,)), ((), ())), preferred_element_type=F32)
        column = jnp.broadcast_to(offall[j], (128, r)).T
        s = s + column[:, :1]
        top = jnp.max(s, axis=0, keepdims=True)
        e = jnp.exp(s - top)
        ebuf[j, i, :, cols] = e
        peak[j, hh, i] = top
        blk_lse[j, hh, i] = top + jnp.log(jnp.sum(e, axis=0, keepdims=True))

    @pl.loop(0, tiles // TILES)
    def _(u):
        @pl.when(u == pair[1])
        def _():
            for v in range((n_ca - 3) * halves):
                event(v)
            images_in(0)

        @pl.when(u == pair[2])
        def _():
            paired(3, bx, 0)
            paired(4, by, 0)

        @pl.when(u == pair[3])
        def _():
            for v in range((n_ca - 3) * halves, (n_ca - 2) * halves):
                event(v)
            images_in(1)

        @pl.when(u == pair[5])
        def _():
            paired(3, bx, 1)
            paired(4, by, 1)

        @pl.when(u == pair[6] - 1)
        def _():
            corner_in(0)

        @pl.when(u == pair[6])
        def _():
            paired(5, bd, 0)

        @pl.when(u == pair[7])
        def _():
            for v in range((n_ca - 2) * halves, events):
                event(v)

        @pl.when(u == pair[7] + 1)
        def _():
            corner_in(1)

        @pl.when(u == pair[8])
        def _():
            paired(5, bd, 1)

        @pl.when(u == pair[8] + 1)
        def _():
            reduce_lse(0)

        @pl.when(u == pair[8] + 2)
        def _():
            share_lse(0)

        for w in range(TILES):
            tile(TILES * u + w)

    reduce_lse(1)
    logits = logits_ref[...]
    top = jnp.max(jnp.max(logits, axis=0), axis=1, keepdims=True)
    logit_total = top + jnp.log(jnp.sum(jnp.sum(jnp.exp(logits - top[None]), axis=0), axis=1, keepdims=True))

    def finish_lse(hh):
        @pl.loop(1, n)
        def _(k):
            send_lse(k, hh).wait_recv()

        own_lse = lse[hh]
        high = lax.fori_loop(1, n, lambda k, h: jnp.maximum(h, lbuf[k, hh]), own_lse)
        total = lax.fori_loop(1, n, lambda k, x: x + jnp.exp(lbuf[k, hh] - high), jnp.exp(own_lse - high))
        row_total = high + jnp.log(total)
        tot[hh] = row_total
        like_ref[:, hh * part_rows:(hh + 1) * part_rows] = tot[hh, b] - logit_total

        @pl.loop(0, n_ca)
        def _(j):
            peak[j, hh] = jnp.exp(peak[j, hh] - row_total)

    share_lse(1)
    finish_lse(0)

    def info(k):
        j = target(k, a, n_ca)
        way = (j < a).astype(jnp.int32)
        joined = jnp.where(j < a, a < n_ca - 1, a > 0)
        return j, way, joined

    def slot(j, way, owner):
        return jnp.where(jnp.logical_and(j == owner, way == 1), n_ca, j)

    def out_copies(k, h):
        j, way, _ = info(k)
        nbr = jnp.clip(a + 1 - 2 * way, 0, n_ca - 1)
        dev = (nbr, b, m)
        s = slot(j, way, nbr)
        rows = pl.ds(pl.multiple_of(h * rh, rh), rh)
        return (
            remote(sbuf.at[j, rows], rbuf.at[s, rows], msend.at[j, h], mrecv.at[s, h], dev),
            remote(sc.at[j, h], rc.at[s, h], csend.at[j, h], crecv.at[s, h], dev),
        )

    def in_copies(j, way, h):
        nbr = jnp.clip(a - 1 + 2 * way, 0, n_ca - 1)
        dev = (nbr, b, m)
        s = slot(j, way, a)
        rows = pl.ds(pl.multiple_of(h * rh, rh), rh)
        return s, (
            remote(sbuf.at[j, rows], rbuf.at[s, rows], msend.at[j, h], mrecv.at[s, h], dev),
            remote(sc.at[j, h], rc.at[s, h], csend.at[j, h], crecv.at[s, h], dev),
        )

    def start_piece(v):
        for c in out_copies(v // halves, lax.rem(v, halves)):
            c.start()

    def merge(v):
        k, h = v // halves, lax.rem(v, halves)
        j, way, _ = info(k)
        s, copies = in_copies(j, way, h)
        for c in copies:
            c.wait_recv()
        rows = pl.ds(pl.multiple_of(h * rh, rh), rh)
        sbuf[j, rows] = (acc[k, rows] + rbuf[s, rows].astype(F32)).astype(BF16)
        sc[j, h] = crow[k, h] + rc[s, h]

    exports = (n_ca - 1) * halves

    def flush(v):
        @pl.when(jnp.logical_and(jnp.logical_and(v >= 1, v - 1 < exports), jnp.logical_not(info((v - 1) // halves)[2])))
        def _():
            start_piece(jnp.maximum(v - 1, 0))

        w = v - 1 - halves

        @pl.when(jnp.logical_and(w >= 0, info(jnp.maximum(w, 0) // halves)[2]))
        def _():
            start_piece(jnp.maximum(w, 0))

    def weigh(k, h, hh):
        j = target(k, a, n_ca)
        rows = pl.ds(pl.multiple_of(h * rh, rh), rh)
        cols = pl.ds(hh * part_rows, part_rows)
        prod = part = None
        for i in range(SQUARE):
            shares = (ebuf[j, i, rows, cols] * peak[j, hh, i]).astype(BF16)
            wide = shares.astype(F32)
            for q in range(part_rows // 128):
                lane = wide[:, q * 128:(q + 1) * 128]
                part = lane if part is None else part + lane
            p = jnp.dot(shares, feats[i, cols], preferred_element_type=F32)
            prod = p if prod is None else prod + p
        return prod, part

    def settle(v, k, h):
        rows = pl.ds(pl.multiple_of(h * rh, rh), rh)
        crow[k, h] = jnp.sum(cacc[...].T, axis=0, keepdims=True)

        @pl.when(jnp.logical_and(v < exports, jnp.logical_not(info(k)[2])))
        def _():
            j = info(k)[0]
            sbuf[j, rows] = acc[k, rows].astype(BF16)
            sc[j, h] = crow[k, h]

        w = v - halves

        @pl.when(jnp.logical_and(w >= 0, info(jnp.maximum(w, 0) // halves)[2]))
        def _():
            merge(jnp.maximum(w, 0))

    acc[0, :rh], cacc[...] = weigh(0, 0, 0)
    finish_lse(1)
    prod, part = weigh(0, 0, 1)
    acc[0, :rh] += prod
    cacc[...] += part
    settle(0, 0, 0)

    @pl.loop(1, n_ca * halves)
    def _(v):
        k, h = v // halves, lax.rem(v, halves)
        rows = pl.ds(pl.multiple_of(h * rh, rh), rh)
        prod, part = weigh(k, h, 0)
        acc[k, rows] = prod
        cacc[...] = part
        flush(v)
        prod, part = weigh(k, h, 1)
        acc[k, rows] += prod
        cacc[...] += part
        settle(v, k, h)

    first_ref[...] = acc[n_ca - 1, :, d:] + means_ref[...]
    second_ref[...] = acc[n_ca - 1, :, :d] + 1.0 / prec_ref[...] + means_ref[...] * means_ref[...]
    flush(n_ca * halves)

    def join(way, h):
        s, copies = in_copies(a, jnp.int32(way), h)
        for c in copies:
            c.wait_recv()
        rows = pl.ds(h * rh, rh)
        first_ref[rows] += rbuf[s, rows, d:].astype(F32)
        second_ref[rows] += rbuf[s, rows, :d].astype(F32)
        crow[n_ca - 1, h] += rc[s, h]

    for h in range(halves):
        @pl.when(a > 0)
        def _():
            join(0, h)

        @pl.when(a < n_ca - 1)
        def _():
            join(1, h)

    for h in range(halves):
        den_ref[h] = crow[n_ca - 1, h] + 1.0

    @pl.loop(0, exports)
    def _(v):
        for c in out_copies(v // halves, lax.rem(v, halves)):
            c.wait_send()

    for k, i in enumerate((b, b, bd, bx, by, bd)):
        for piece in range(PIECES):
            img_copy(k, i, to_p, piece).wait_send()

    for dist in range(n_ca - 1):
        for way in (0, 1):
            @pl.when(jnp.logical_and(exists(way, dist), has_next(way)))
            def _():
                for h in range(halves):
                    w_copy(way, dist, h, a).wait_send()
                off_copy(way, dist, a).wait_send()

    @pl.loop(1, n)
    def _(k):
        for hh in range(PIECES):
            send_lse(k, hh).wait_send()


def em(images, means, precisions, logits, n_ca, n_mp):
    t, d = images.shape
    r = means.shape[0]
    halves = 2 if r % 32 == 0 else 1
    n = SQUARE * n_mp
    vmem = pl.BlockSpec(memory_space=pltpu.VMEM)
    dma = pltpu.SemaphoreType.DMA
    line = dma((2, n_ca - 1, halves))
    short = dma((2, n_ca - 1))
    return pl.pallas_call(
        functools.partial(em_kernel, n_ca, n_mp, halves),
        out_shape=(
            jax.ShapeDtypeStruct((r, d), F32),
            jax.ShapeDtypeStruct((r, d), F32),
            jax.ShapeDtypeStruct((halves, 1, r // halves), F32),
            jax.ShapeDtypeStruct((1, t), F32),
        ),
        in_specs=[pl.BlockSpec(memory_space=pl.ANY), vmem, vmem, vmem],
        out_specs=(vmem,) * 4,
        scratch_shapes=[
            pltpu.VMEM((SQUARE, t, 2 * d), BF16),
            pltpu.VMEM((n_ca, r, 2 * d), BF16),
            pltpu.VMEM((n_ca, 1, r), F32),
            pltpu.VMEM((n_ca, SQUARE, r, t), F32),
            pltpu.VMEM((n_ca, PIECES, SQUARE, 1, t // PIECES), F32),
            pltpu.VMEM((n_ca, PIECES, SQUARE, 1, t // PIECES), F32),
            pltpu.VMEM((PIECES, SQUARE, 1, t // PIECES), F32),
            pltpu.VMEM((PIECES, SQUARE, 1, t // PIECES), F32),
            pltpu.VMEM((n, PIECES, SQUARE, 1, t // PIECES), F32),
            pltpu.VMEM((n_ca, r, 2 * d), F32),
            pltpu.VMEM((r // halves, 128), F32),
            pltpu.VMEM((n_ca, halves, 1, r // halves), F32),
            pltpu.VMEM((n_ca, r, 2 * d), BF16),
            pltpu.VMEM((n_ca, halves, 1, r // halves), F32),
            pltpu.VMEM((n_ca + 1, r, 2 * d), BF16),
            pltpu.VMEM((n_ca + 1, halves, 1, r // halves), F32),
            dma((1,)),
            dma((6, PIECES)),
            dma((6, PIECES)),
            line, line, short, short,
            dma((n, PIECES)),
            dma((n, PIECES)),
            dma((n_ca, halves)),
            dma((n_ca + 1, halves)),
            dma((n_ca, halves)),
            dma((n_ca + 1, halves)),
        ],
        compiler_params=pltpu.CompilerParams(
            collective_id=0, has_side_effects=True, vmem_limit_bytes=VMEM_LIMIT
        ),
        name="em",
    )(images, means, precisions, logits.reshape(-1, 1, r))


def body(n_ca, n_mp, images, means, precisions, logits):
    t, d = images.shape
    r = means.shape[0]
    first, second, denominator, like = em(images, means, precisions, logits, n_ca, n_mp)
    denominator = denominator.reshape(r)
    total = float(t * n_ca * SQUARE + logits.shape[0])
    new_means = first / denominator[:, None]
    new_variances = second / denominator[:, None] - new_means * new_means
    new_log_weights = jnp.log(denominator) - jnp.log(jnp.float32(total))
    return (new_means, new_variances, new_log_weights, like[0])


def solution(mesh):
    n_dp, n_mp = mesh.shape["dp"], mesh.shape["mp"]
    n_ca = n_dp // SQUARE
    split = Mesh(mesh.devices.reshape(n_ca, SQUARE, n_mp), ("ca", "ib", "mp"))
    dp = ("ca", "ib")
    comp = ("mp", "ca", "ib")
    return jax.shard_map(
        functools.partial(body, n_ca, n_mp),
        mesh=split,
        in_specs=(P(dp, None), P(comp, None), P(comp, None), P()),
        out_specs=(P(comp, None), P(comp, None), P(comp), P(dp)),
        check_vma=False,
    )
```

time: 114 us -> 81.7 us (0.72); the launches traced: 113 us -> 81.6 us
  Pallas kernels: 103 us -> 77.6 us
  other arithmetic: 7.81 us -> 2.7 us
    pallas_call x3 -> x1, Pallas kernels: 103 us -> 77.6 us  [em(): pl.pallas_call(functools.partial(em_kernel, n_ca, n_mp, halves), out_shap...]
    sub x1 -> x0, other arithmetic: 1.33 us -> none  [body(): own_logits + 0.5 * jnp.sum(jnp.log(precisions) - means * means * precisio...]
    dynamic_slice x1 -> x0, local copies, waits for them, and re-layouts: 1.29 us -> none  [body(): log_likelihood = lax.dynamic_slice_in_dim(like[0], b * t, t)]
    reduce_sum x1 -> x0, other arithmetic: 1.29 us -> none  [body(): jnp.sum(jnp.log(precisions) - means * means * precisions, axis=1)]
where the time goes in v1:
time: 81.7 us; the launch traced here: 81.6 us
  Pallas kernels  77.6 us (95%)
  other arithmetic  2.7 us (3%)
    pallas_call x1, Pallas kernels, em(): pl.pallas_call(functools.partial(em_kernel, n_ca, n_mp, halves), out_shap...  77.6 us
    sub x1, other arithmetic, body(): new_variances = second / denominator[:, None] - new_means * new_means  2.13 us

profile of v1, /device:TPU:16, one launch (start us, length us, event | category | flops | bytes accessed | tf_op | source)
XLA Modules:
  0.0 81.6 jit_solution(17825562019402716553)
XLA Ops:
  0.6 77.6 %em.1 = (f32[256,384]{1,0:T(8,128)}, f32[256,384]{1,0:T(8,128)}, f32[2,1,128]{2,1,0:T(1,128)}, f32[1,2048]{1,0:T(1,128)}) custom-call(bf16[2048,384]{1,0:T(8,128)(2,1)} %img_ref.1, f32[256,384]{1,0:T(8,128)} %means_ref.1, f32[256,384]{1,0:T(8,128)} %prec_ref.1, f32[32,1,256]{2,1,0:T(1,128)} %bitcast.3), custom_call_target="tpu_custom_call" | custom-call | tf_op jit(solution)/shard_map/em/pallas_call | solution.py:481
  78.2 0.0 copy-start.1
  78.3 0.0 copy-start
  78.3 2.1 %multiply_subtract_fusion = (f32[256,384]{1,0:T(8,128)}, f32[256,384]{1,0:T(8,128)}) fusion(f32[256,384]{1,0:T(8,128)} %get-tuple-element.10, f32[256]{0:T(256)} %bitcast.5, f32[256,384]{1,0:T(8,128)} %get-tuple-element.8), kind=kLoop, calls=%fused_computation | loop fusion | flops 393216 | bytes 1573888 | tf_op jit(solution)/shard_map/sub | solution.py:533
  80.4 0.0 copy-done.1
  80.4 0.6 log_add_fusion
  81.0 0.0 copy-done
  81.0 0.6 copy.9
Async XLA Ops:
  78.2 2.2 %copy-start.1 = (f32[2,1,128]{2,1,0:T(1,128)S(1)}, f32[2,1,128]{2,1,0:T(1,128)}, u32[]{:S(2)}) copy-start(f32[2,1,128]{2,1,0:T(1,128)} %get-tuple-element.9) | copy-start | bytes 3076
  78.3 2.7 %copy-start = (f32[1,2048]{1,0:T(1,128)S(1)}, f32[1,2048]{1,0:T(1,128)}, u32[]{:S(2)}) copy-start(f32[1,2048]{1,0:T(1,128)} %get-tuple-element.11) | copy-start | bytes 24580

commit v2 on v1

--- a/solution.py
+++ b/solution.py
@@ -36,7 +36,7 @@
 
 def schedule(n_ca):
     b, c = n_ca - 2, n_ca - 1
-    both, near, far, early, late = (0, 4), (1, 1), (5, 1), (0, 1), (4, 1)
+    both, near, far = (0, 4), (1, 1), (5, 1)
     shapes = (
         (0, 1, both, 2),
         (1, b, both, 2),
@@ -44,10 +44,6 @@
         (b, c, both, 2),
         (b, c, near, 2),
         (0, c, far, 2),
-        (0, c, (3, 1), 1),
-        (c, n_ca, early, 4),
-        (0, c, (7, 1), 1),
-        (c, n_ca, late, 4),
     )
     out, t = [], 0
     for q0, q1, (p0, stride), count in shapes:
@@ -58,7 +54,7 @@
 
 def em_kernel(n_ca, n_mp, halves, img_ref, means_ref, prec_ref, logits_ref,
               first_ref, second_ref, den_ref, like_ref,
-              feats, wall, offall, ebuf, peak, blk_lse, lse, tot, lbuf, acc, cacc, crow, sbuf, sc, rbuf, rc,
+              feats, wall, offall, offcol, ebuf, peak, blk_lse, lse, tot, lbuf, acc, cacc, crow, sbuf, sc, rbuf, rc,
               loc, isend, irecv, wsend, wrecv, osend, orecv, lsend, lrecv, msend, mrecv, csend, crecv):
     a, b, m = lax.axis_index("ca"), lax.axis_index("ib"), lax.axis_index("mp")
     t_rows, d = img_ref.shape
@@ -147,6 +143,9 @@
         for way in (0, 1):
             forward(way, 0, h)
 
+    def column(blk):
+        offcol[blk] = jnp.broadcast_to(offall[blk], (128, r)).T
+
     def event(u):
         dist, h = u // halves + 1, u % halves
         for way in (0, 1):
@@ -158,6 +157,8 @@
                     off_copy(way, dist - 1, sender).wait_recv()
                 if dist < n_ca - 1:
                     forward(way, dist, h)
+                if h == 0:
+                    column(hop(way, dist - 1, sender)[0])
 
     def images_in(piece):
         img_copy(0, bx, to_x, piece).wait_recv()
@@ -188,6 +189,7 @@
         square(i, piece)
 
     own.wait()
+    column(a)
     for piece in range(PIECES):
         square(b, piece)
 
@@ -213,25 +215,27 @@
     pair = [x[0] // TILES for x in rects]
     events = (n_ca - 1) * halves
 
-    def tile(t):
+    def tile(q, p, hh):
+        j = target(n_ca - 1 - q, a, n_ca)
+        i = shard(p)
+        cols = pl.ds(pl.multiple_of(hh * part_rows, part_rows), part_rows)
+        s = lax.dot_general(wall[j], feats[i, cols], (((1,), (1,)), ((), ())), preferred_element_type=F32)
+        s = s + offcol[j][:, :1]
+        top = jnp.max(s, axis=0, keepdims=True)
+        e = jnp.exp(s - top)
+        ebuf[j, i, :, cols] = e
+        peak[j, hh, i] = top
+        blk_lse[j, hh, i] = top + jnp.log(jnp.sum(e, axis=0, keepdims=True))
+
+    def early_tile(t):
         q, part = t, t
         for t0, q0, p0, stride, count in rects:
             here = t >= t0
             s = jnp.maximum(t - t0, 0)
             q = jnp.where(here, q0 + s // count, q)
             part = jnp.where(here, p0 + stride * lax.rem(s, count), part)
-        j = target(n_ca - 1 - q, a, n_ca)
         hh = part // SQUARE
-        i = shard(part - SQUARE * hh)
-        cols = pl.ds(pl.multiple_of(hh * part_rows, part_rows), part_rows)
-        s = lax.dot_general(wall[j], feats[i, cols], (((1,), (1,)), ((), ())), preferred_element_type=F32)
-        column = jnp.broadcast_to(offall[j], (128, r)).T
-        s = s + column[:, :1]
-        top = jnp.max(s, axis=0, keepdims=True)
-        e = jnp.exp(s - top)
-        ebuf[j, i, :, cols] = e
-        peak[j, hh, i] = top
-        blk_lse[j, hh, i] = top + jnp.log(jnp.sum(e, axis=0, keepdims=True))
+        tile(q, part - SQUARE * hh, hh)
 
     @pl.loop(0, tiles // TILES)
     def _(u):
@@ -257,37 +261,43 @@
             paired(3, bx, 1)
             paired(4, by, 1)
 
-        @pl.when(u == pair[6] - 1)
+        @pl.when(u == tiles // TILES - 1)
         def _():
             corner_in(0)
 
-        @pl.when(u == pair[6])
+        for w in range(TILES):
+            early_tile(TILES * u + w)
+
+    group = 3 if (n_ca - 1) % 3 == 0 else 1
+
+    @pl.loop(0, PIECES)
+    def _(hh):
+        @pl.when(hh == 0)
         def _():
             paired(5, bd, 0)
 
-        @pl.when(u == pair[7])
+        @pl.when(hh == 1)
+        def _():
+            paired(5, bd, 1)
+            reduce_lse(0)
+
+        @pl.loop(0, (n_ca - 1) // group)
+        def _(u):
+            for w in range(group):
+                tile(group * u + w, SQUARE - 1, hh)
+
+        @pl.when(hh == 0)
         def _():
             for v in range((n_ca - 2) * halves, events):
                 event(v)
-
-        @pl.when(u == pair[7] + 1)
-        def _():
             corner_in(1)
 
-        @pl.when(u == pair[8])
-        def _():
-            paired(5, bd, 1)
-
-        @pl.when(u == pair[8] + 1)
-        def _():
-            reduce_lse(0)
-
-        @pl.when(u == pair[8] + 2)
+        @pl.when(hh == 1)
         def _():
             share_lse(0)
 
-        for w in range(TILES):
-            tile(TILES * u + w)
+        for p in range(SQUARE):
+            tile(n_ca - 1, p, hh)
 
     reduce_lse(1)
     logits = logits_ref[...]
@@ -412,10 +422,10 @@
     def _(v):
         k, h = v // halves, lax.rem(v, halves)
         rows = pl.ds(pl.multiple_of(h * rh, rh), rh)
+        flush(v)
         prod, part = weigh(k, h, 0)
         acc[k, rows] = prod
         cacc[...] = part
-        flush(v)
         prod, part = weigh(k, h, 1)
         acc[k, rows] += prod
         cacc[...] += part
@@ -492,6 +502,7 @@
             pltpu.VMEM((SQUARE, t, 2 * d), BF16),
             pltpu.VMEM((n_ca, r, 2 * d), BF16),
             pltpu.VMEM((n_ca, 1, r), F32),
+            pltpu.VMEM((n_ca, r, 128), F32),
             pltpu.VMEM((n_ca, SQUARE, r, t), F32),
             pltpu.VMEM((n_ca, PIECES, SQUARE, 1, t // PIECES), F32),
             pltpu.VMEM((n_ca, PIECES, SQUARE, 1, t // PIECES), F32),
@@ -523,16 +534,37 @@
     )(images, means, precisions, logits.reshape(-1, 1, r))
 
 
+def finish_kernel(total, first_ref, second_ref, den_ref, like_ref, nm_ref, nv_ref, nw_ref, ll_ref):
+    halves, _, rh = den_ref.shape
+    for h in range(halves):
+        rows = slice(h * rh, (h + 1) * rh)
+        den = den_ref[h]
+        inv = 1.0 / jnp.broadcast_to(den, (128, rh)).T[:, :1]
+        mean = first_ref[rows] * inv
+        nm_ref[rows] = mean
+        nv_ref[rows] = second_ref[rows] * inv - mean * mean
+        nw_ref[h] = jnp.log(den) - jnp.log(jnp.float32(total))
+    ll_ref[...] = like_ref[...]
+
+
+def finish(total, first, second, den, like):
+    vmem = pl.BlockSpec(memory_space=pltpu.VMEM)
+    return pl.pallas_call(
+        functools.partial(finish_kernel, total),
+        out_shape=tuple(jax.ShapeDtypeStruct(x.shape, F32) for x in (first, second, den, like)),
+        in_specs=[vmem] * 4,
+        out_specs=(vmem,) * 4,
+        name="finish",
+    )(first, second, den, like)
+
+
 def body(n_ca, n_mp, images, means, precisions, logits):
     t, d = images.shape
     r = means.shape[0]
-    first, second, denominator, like = em(images, means, precisions, logits, n_ca, n_mp)
-    denominator = denominator.reshape(r)
     total = float(t * n_ca * SQUARE + logits.shape[0])
-    new_means = first / denominator[:, None]
-    new_variances = second / denominator[:, None] - new_means * new_means
-    new_log_weights = jnp.log(denominator) - jnp.log(jnp.float32(total))
-    return (new_means, new_variances, new_log_weights, like[0])
+    outs = em(images, means, precisions, logits, n_ca, n_mp)
+    new_means, new_variances, new_log_weights, like = finish(total, *outs)
+    return (new_means, new_variances, new_log_weights.reshape(r), like[0])
 
 
 def solution(mesh):

time: 81.7 us -> 76.2 us (0.933)
  other arithmetic: 2.7 us -> 0 us
  Pallas kernels: 77.6 us -> 75.2 us
    pallas_call x1, Pallas kernels: 77.6 us -> 73 us  [em(): pl.pallas_call(functools.partial(em_kernel, n_ca, n_mp, halves), out_shap...]
    sub x2 -> x0, other arithmetic: 2.7 us -> none  [the longest x1 2.13 us: body(): new_variances = second / denominator[:, None] - new_means * new_means]
    pallas_call x0 -> x1, Pallas kernels: none -> 2.2 us  [finish(): pl.pallas_call(functools.partial(finish_kernel, total), out_shape=tuple((...]
where the time goes in v2:
time: 76.2 us; the launch traced here: 75.9 us
  Pallas kernels  75.2 us (99%)
    pallas_call x1, Pallas kernels, em(): pl.pallas_call(functools.partial(em_kernel, n_ca, n_mp, halves), out_shap...  73 us
    pallas_call x1, Pallas kernels, finish(): pl.pallas_call(functools.partial(finish_kernel, total), out_shape=tuple((...  2.2 us

profile of v2, /device:TPU:16, one launch (start us, length us, event | category | flops | bytes accessed | tf_op | source)
XLA Modules:
  0.0 75.9 jit_solution(5424896203071962876)
XLA Ops:
  0.6 73.0 %em.1 = (f32[256,384]{1,0:T(8,128)}, f32[256,384]{1,0:T(8,128)}, f32[2,1,128]{2,1,0:T(1,128)}, f32[1,2048]{1,0:T(1,128)}) custom-call(bf16[2048,384]{1,0:T(8,128)(2,1)} %img_ref.1, f32[256,384]{1,0:T(8,128)} %means_ref.1, f32[256,384]{1,0:T(8,128)} %prec_ref.1, f32[32,1,256]{2,1,0:T(1,128)} %bitcast.3), custom_call_target="tpu_custom_call" | custom-call | tf_op jit(solution)/shard_map/em/pallas_call | solution.py:491
  73.7 2.2 %finish.1 = (f32[256,384]{1,0:T(8,128)}, f32[256,384]{1,0:T(8,128)}, f32[2,1,128]{2,1,0:T(1,128)}, f32[1,2048]{1,0:T(1,128)}) custom-call(f32[256,384]{1,0:T(8,128)} %get-tuple-element.12.first_ref, f32[256,384]{1,0:T(8,128)} %get-tuple-element.13.second_ref, f32[2,1,128]{2,1,0:T(1,128)} %get-tuple-element.14.den_ref, f32[1,2048]{1,0:T(1,128)} %get-tuple-element.15.like_ref), custom_call_target="tpu_custom_call" | custom-call | tf_op jit(solution)/shard_map/finish/pallas_call | solution.py:552

commit v3 on v2

--- a/solution.py
+++ b/solution.py
@@ -14,7 +14,7 @@
 TILES = 2
 F32 = jnp.float32
 BF16 = jnp.bfloat16
-VMEM_LIMIT = 67_043_328
+VMEM_LIMIT = 65_500_000
 
 
 def remote(src, dst, send, recv, device):
@@ -52,13 +52,13 @@
     return out, t
 
 
-def em_kernel(n_ca, n_mp, halves, img_ref, means_ref, prec_ref, logits_ref,
+def em_kernel(n_ca, n_mp, halves, img_ref, means_hbm, prec_hbm, logits_hbm,
               first_ref, second_ref, den_ref, like_ref,
-              feats, wall, offall, offcol, ebuf, peak, blk_lse, lse, tot, lbuf, acc, cacc, crow, sbuf, sc, rbuf, rc,
+              means_ref, prec_ref, logits_ref, feats, wall, offall, offcol, ebuf, peak, blk_lse, lse, tot, lbuf, acc, cacc, crow, sbuf, sc, rbuf, rc,
               loc, isend, irecv, wsend, wrecv, osend, orecv, lsend, lrecv, msend, mrecv, csend, crecv):
     a, b, m = lax.axis_index("ca"), lax.axis_index("ib"), lax.axis_index("mp")
     t_rows, d = img_ref.shape
-    r = means_ref.shape[0]
+    r = means_hbm.shape[0]
     rh = r // halves
     core = lax.rem(m, 2)
     partner = m + 1 - 2 * core
@@ -93,7 +93,16 @@
         return feats.at[i, rows, pl.ds(d, d)]
 
     own = pltpu.make_async_copy(img_ref, feats.at[b, :, pl.ds(d, d)], loc.at[0])
+    fetch = (
+        pltpu.make_async_copy(means_hbm, means_ref, loc.at[1]),
+        pltpu.make_async_copy(prec_hbm, prec_ref, loc.at[2]),
+        pltpu.make_async_copy(logits_hbm, logits_ref, loc.at[3]),
+    )
+    for c in fetch:
+        c.start()
     own.start()
+    for c in fetch:
+        c.wait()
 
     means, prec = means_ref[...], prec_ref[...]
     wall[a] = jnp.concatenate([-0.5 * prec.astype(BF16), (means * prec).astype(BF16)], axis=1)
@@ -199,12 +208,12 @@
     def send_lse(k, hh):
         return remote(lse.at[hh], lbuf.at[k, hh], lsend.at[k, hh], lrecv.at[k, hh], peer(k))
 
+    def log_sum(rows):
+        high = functools.reduce(jnp.maximum, rows)
+        return high + jnp.log(functools.reduce(jnp.add, [jnp.exp(x - high) for x in rows]))
+
     def reduce_lse(hh):
-        high = lax.fori_loop(1, n_ca, lambda k, h: jnp.maximum(h, blk_lse[k, hh]), blk_lse[0, hh])
-        tot = lax.fori_loop(
-            1, n_ca, lambda k, x: x + jnp.exp(blk_lse[k, hh] - high), jnp.exp(blk_lse[0, hh] - high)
-        )
-        lse[hh] = high + jnp.log(tot)
+        lse[hh] = log_sum([blk_lse[k, hh] for k in range(n_ca)])
 
     def share_lse(hh):
         @pl.loop(1, n)
@@ -299,29 +308,16 @@
         for p in range(SQUARE):
             tile(n_ca - 1, p, hh)
 
-    reduce_lse(1)
-    logits = logits_ref[...]
-    top = jnp.max(jnp.max(logits, axis=0), axis=1, keepdims=True)
-    logit_total = top + jnp.log(jnp.sum(jnp.sum(jnp.exp(logits - top[None]), axis=0), axis=1, keepdims=True))
-
     def finish_lse(hh):
         @pl.loop(1, n)
         def _(k):
             send_lse(k, hh).wait_recv()
 
-        own_lse = lse[hh]
-        high = lax.fori_loop(1, n, lambda k, h: jnp.maximum(h, lbuf[k, hh]), own_lse)
-        total = lax.fori_loop(1, n, lambda k, x: x + jnp.exp(lbuf[k, hh] - high), jnp.exp(own_lse - high))
-        row_total = high + jnp.log(total)
-        tot[hh] = row_total
-        like_ref[:, hh * part_rows:(hh + 1) * part_rows] = tot[hh, b] - logit_total
-
-        @pl.loop(0, n_ca)
-        def _(j):
-            peak[j, hh] = jnp.exp(peak[j, hh] - row_total)
-
+        tot[hh] = log_sum([lse[hh]] + [lbuf[k, hh] for k in range(1, n)])
+
+    reduce_lse(1)
+    finish_lse(0)
     share_lse(1)
-    finish_lse(0)
 
     def info(k):
         j = target(k, a, n_ca)
@@ -386,7 +382,8 @@
         cols = pl.ds(hh * part_rows, part_rows)
         prod = part = None
         for i in range(SQUARE):
-            shares = (ebuf[j, i, rows, cols] * peak[j, hh, i]).astype(BF16)
+            factor = jnp.exp(peak[j, hh, i] - tot[hh, i])
+            shares = (ebuf[j, i, rows, cols] * factor).astype(BF16)
             wide = shares.astype(F32)
             for q in range(part_rows // 128):
                 lane = wide[:, q * 128:(q + 1) * 128]
@@ -435,6 +432,12 @@
     second_ref[...] = acc[n_ca - 1, :, :d] + 1.0 / prec_ref[...] + means_ref[...] * means_ref[...]
     flush(n_ca * halves)
 
+    logits = logits_ref[...]
+    top = jnp.max(jnp.max(logits, axis=0), axis=1, keepdims=True)
+    logit_total = top + jnp.log(jnp.sum(jnp.sum(jnp.exp(logits - top[None]), axis=0), axis=1, keepdims=True))
+    for hh in range(PIECES):
+        like_ref[:, hh * part_rows:(hh + 1) * part_rows] = tot[hh, b] - logit_total
+
     def join(way, h):
         s, copies = in_copies(a, jnp.int32(way), h)
         for c in copies:
@@ -491,14 +494,17 @@
     return pl.pallas_call(
         functools.partial(em_kernel, n_ca, n_mp, halves),
         out_shape=(
-            jax.ShapeDtypeStruct((r, d), F32),
-            jax.ShapeDtypeStruct((r, d), F32),
-            jax.ShapeDtypeStruct((halves, 1, r // halves), F32),
-            jax.ShapeDtypeStruct((1, t), F32),
+            pltpu.VMEM((r, d), F32),
+            pltpu.VMEM((r, d), F32),
+            pltpu.VMEM((halves, 1, r // halves), F32),
+            pltpu.VMEM((1, t), F32),
         ),
-        in_specs=[pl.BlockSpec(memory_space=pl.ANY), vmem, vmem, vmem],
+        in_specs=[pl.BlockSpec(memory_space=pl.ANY)] * 4,
         out_specs=(vmem,) * 4,
         scratch_shapes=[
+            pltpu.VMEM((r, d), F32),
+            pltpu.VMEM((r, d), F32),
+            pltpu.VMEM((logits.shape[0] // r, 1, r), F32),
             pltpu.VMEM((SQUARE, t, 2 * d), BF16),
             pltpu.VMEM((n_ca, r, 2 * d), BF16),
             pltpu.VMEM((n_ca, 1, r), F32),
@@ -516,7 +522,7 @@
             pltpu.VMEM((n_ca, halves, 1, r // halves), F32),
             pltpu.VMEM((n_ca + 1, r, 2 * d), BF16),
             pltpu.VMEM((n_ca + 1, halves, 1, r // halves), F32),
-            dma((1,)),
+            dma((4,)),
             dma((6, PIECES)),
             dma((6, PIECES)),
             line, line, short, short,
@@ -555,7 +561,7 @@
         in_specs=[vmem] * 4,
         out_specs=(vmem,) * 4,
         name="finish",
-    )(first, second, den, like)
+    )(*(pltpu.with_memory_space_constraint(x, pltpu.VMEM) for x in (first, second, den, like)))
 
 
 def body(n_ca, n_mp, images, means, precisions, logits):

time: 76.2 us -> 74.2 us (0.974)
  Pallas kernels: 75.2 us -> 73.3 us
    pallas_call x1, Pallas kernels: 2.2 us -> 1.08 us  [finish(): pl.pallas_call(functools.partial(finish_kernel, total), out_shape=tuple((...]
    pallas_call x1, Pallas kernels: 73 us -> 72.2 us  [em(): pl.pallas_call(functools.partial(em_kernel, n_ca, n_mp, halves), out_shap...]
where the time goes in v3:
time: 74.2 us; the launch traced here: 73.9 us
  Pallas kernels  73.3 us (99%)
    pallas_call x1, Pallas kernels, em(): pl.pallas_call(functools.partial(em_kernel, n_ca, n_mp, halves), out_shap...  72.2 us

profile of v3, /device:TPU:16, one launch (start us, length us, event | category | flops | bytes accessed | tf_op | source)
XLA Modules:
  0.0 73.9 jit_solution(12705551626174506814)
XLA Ops:
  0.6 72.2 %em.1 = (f32[256,384]{1,0:T(8,128)S(1)}, f32[256,384]{1,0:T(8,128)S(1)}, f32[2,1,128]{2,1,0:T(1,128)S(1)}, f32[1,2048]{1,0:T(1,128)S(1)}) custom-call(bf16[2048,384]{1,0:T(8,128)(2,1)} %img_ref.1, f32[256,384]{1,0:T(8,128)} %means_hbm.1, f32[256,384]{1,0:T(8,128)} %prec_hbm.1, f32[32,1,256]{2,1,0:T(1,128)} %bitcast.3), custom_call_target="tpu_custom_call" | custom-call | tf_op jit(solution)/shard_map/em/pallas_call | solution.py:494
  72.9 1.1 %finish.1 = (f32[256,384]{1,0:T(8,128)}, f32[256,384]{1,0:T(8,128)}, f32[2,1,128]{2,1,0:T(1,128)}, f32[1,2048]{1,0:T(1,128)}) custom-call(f32[256,384]{1,0:T(8,128)S(1)} %get-tuple-element.12.first_ref, f32[256,384]{1,0:T(8,128)S(1)} %get-tuple-element.13.second_ref, f32[2,1,128]{2,1,0:T(1,128)S(1)} %get-tuple-element.14.den_ref, ...), custom_call_target="tpu_custom_call" | custom-call | tf_op jit(solution)/shard_map/finish/pallas_call | solution.py:558

commit v4 on v3

--- a/solution.py
+++ b/solution.py
@@ -278,6 +278,7 @@
             early_tile(TILES * u + w)
 
     group = 3 if (n_ca - 1) % 3 == 0 else 1
+    square_tail = n_ca == SQUARE
 
     @pl.loop(0, PIECES)
     def _(hh):
@@ -287,13 +288,20 @@
 
         @pl.when(hh == 1)
         def _():
-            paired(5, bd, 1)
+            if not square_tail:
+                paired(5, bd, 1)
             reduce_lse(0)
+
+        def tail(q, p):
+            if square_tail:
+                first = hh == 0
+                q, p = jnp.where(first, q, p), jnp.where(first, p, q)
+            tile(q, p, hh)
 
         @pl.loop(0, (n_ca - 1) // group)
         def _(u):
             for w in range(group):
-                tile(group * u + w, SQUARE - 1, hh)
+                tail(group * u + w, SQUARE - 1)
 
         @pl.when(hh == 0)
         def _():
@@ -304,9 +312,11 @@
         @pl.when(hh == 1)
         def _():
             share_lse(0)
+            if square_tail:
+                paired(5, bd, 1)
 
         for p in range(SQUARE):
-            tile(n_ca - 1, p, hh)
+            tail(n_ca - 1, p)
 
     def finish_lse(hh):
         @pl.loop(1, n)
@@ -315,9 +325,15 @@
 
         tot[hh] = log_sum([lse[hh]] + [lbuf[k, hh] for k in range(1, n)])
 
+    def sent_lse(hh):
+        @pl.loop(1, n)
+        def _(k):
+            send_lse(k, hh).wait_send()
+
     reduce_lse(1)
+    sent_lse(0)
+    share_lse(1)
     finish_lse(0)
-    share_lse(1)
 
     def info(k):
         j = target(k, a, n_ca)
@@ -476,10 +492,7 @@
                     w_copy(way, dist, h, a).wait_send()
                 off_copy(way, dist, a).wait_send()
 
-    @pl.loop(1, n)
-    def _(k):
-        for hh in range(PIECES):
-            send_lse(k, hh).wait_send()
+    sent_lse(1)
 
 
 def em(images, means, precisions, logits, n_ca, n_mp):

time: 74.2 us -> 72.8 us (0.981)
  Pallas kernels: 73.3 us -> 71.9 us
    pallas_call x1, Pallas kernels: 72.2 us -> 70.8 us  [em(): pl.pallas_call(functools.partial(em_kernel, n_ca, n_mp, halves), out_shap...]
where the time goes in v4:
time: 72.8 us; the launch traced here: 72.5 us
  Pallas kernels  71.9 us (99%)
    pallas_call x1, Pallas kernels, em(): pl.pallas_call(functools.partial(em_kernel, n_ca, n_mp, halves), out_shap...  70.8 us

profile of v4, /device:TPU:16, one launch (start us, length us, event | category | flops | bytes accessed | tf_op | source)
XLA Modules:
  0.0 72.5 jit_solution(10951665293546206652)
XLA Ops:
  0.6 70.8 %em.1 = (f32[256,384]{1,0:T(8,128)S(1)}, f32[256,384]{1,0:T(8,128)S(1)}, f32[2,1,128]{2,1,0:T(1,128)S(1)}, f32[1,2048]{1,0:T(1,128)S(1)}) custom-call(bf16[2048,384]{1,0:T(8,128)(2,1)} %img_ref.1, f32[256,384]{1,0:T(8,128)} %means_hbm.1, f32[256,384]{1,0:T(8,128)} %prec_hbm.1, f32[32,1,256]{2,1,0:T(1,128)} %bitcast.3), custom_call_target="tpu_custom_call" | custom-call | tf_op jit(solution)/shard_map/em/pallas_call | solution.py:507
  71.4 1.1 %finish.1 = (f32[256,384]{1,0:T(8,128)}, f32[256,384]{1,0:T(8,128)}, f32[2,1,128]{2,1,0:T(1,128)}, f32[1,2048]{1,0:T(1,128)}) custom-call(f32[256,384]{1,0:T(8,128)S(1)} %get-tuple-element.12.first_ref, f32[256,384]{1,0:T(8,128)S(1)} %get-tuple-element.13.second_ref, f32[2,1,128]{2,1,0:T(1,128)S(1)} %get-tuple-element.14.den_ref, ...), custom_call_target="tpu_custom_call" | custom-call | tf_op jit(solution)/shard_map/finish/pallas_call | solution.py:571
